TPU v7x, 256 devices: a whole 4x4x8 slice. The times are simulated.
256 devices in a mesh: wide: 32 (over x, y, core), narrow: 8 (over z).
Axes of the slice: x: 4, y: 4, z: 8, core: 2. Of those that a mesh axis runs over, the one named last changes fastest.
Arguments:
- residual: bfloat16 [8192, 4608], P('wide'), may hold values from -6 to 6
- pre_gain: bfloat16 [4608], replicated, may hold values from 0.5 to 1.5
- query_weight: bfloat16 [4608, 4096], P('wide', 'narrow'), may hold values from -0.09375 to 0.09375
- key_weight: bfloat16 [4608, 2048], P('wide', 'narrow'), may hold values from -0.09375 to 0.09375
- value_weight: bfloat16 [4608, 2048], P('wide', 'narrow'), may hold values from -0.09375 to 0.09375
- output_weight: bfloat16 [4096, 4608], P('narrow', 'wide'), may hold values from -1 to 1
- adapter_down: bfloat16 [4608, 768], P('wide', 'narrow'), may hold values from -0.09375 to 0.09375
- adapter_up_query: bfloat16 [256, 4096], P(None, 'narrow'), may hold values from -1.5 to 1.5
- adapter_up_key: bfloat16 [256, 2048], P(None, 'narrow'), may hold values from -1.5 to 1.5
- adapter_up_value: bfloat16 [256, 2048], P(None, 'narrow'), may hold values from -1.5 to 1.5
- adapter_down_out: bfloat16 [4096, 256], P('narrow'), may hold values from -0.09375 to 0.09375
- adapter_up_out: bfloat16 [256, 4608], P(None, 'narrow'), may hold values from -1.5 to 1.5
- post_gain: bfloat16 [4608], P('narrow'), may hold values from 0.5 to 1.5
- sink_logits: float32 [32], P('narrow'), may hold values from -1 to 130
- prompt_lengths: int32 [4], replicated, may hold values from 1 to 4096, 8192 in all
- prompt_adapters: int32 [4], replicated, may hold values from 0 to 15
Outputs:
- layer_out: bfloat16 [8192, 4608], P('wide', 'narrow')
All inputs are finite; a program needn't handle non-finite values.
Results may differ from a plain program's by a relative error of at most 0.022.
Values may be sent and summed in bfloat16 or wider, within the bound.
A program may use at most 128 MiB of HBM per device.

v0:
```python
import jax
import jax.numpy as jnp
from jax import lax
from jax.sharding import PartitionSpec as P

HEAD_DIM = 128
ADAPTERS = 16
epsilon = 1e-06
adapter_scale = 0.5
rotary_base = 10000.0
score_scale = 1.0 / 12.0


def token_layout(prompt_lengths, count, first):
    ends = jnp.cumsum(prompt_lengths, dtype=jnp.int32)
    starts = ends - prompt_lengths
    places = first + jnp.arange(count, dtype=jnp.int32)
    member = jnp.logical_and(
        places[:, None] >= starts[None, :], places[:, None] < ends[None, :]
    ).astype(jnp.int32)
    labels = jnp.arange(prompt_lengths.shape[0], dtype=jnp.int32)
    prompt = jnp.sum(member * labels[None, :], axis=1)
    position = places - jnp.sum(member * starts[None, :], axis=1)
    return (member, prompt, position)


def rotate(values, position):
    half = values.shape[-1] // 2
    exponent = jnp.arange(half, dtype=jnp.float32) * (2.0 / values.shape[-1])
    frequency = jnp.power(jnp.float32(rotary_base), -exponent)
    angle = position.astype(jnp.float32)[:, None] * frequency[None, :]
    cosine = jnp.cos(angle)[:, None, :]
    sine = jnp.sin(angle)[:, None, :]
    first_half = values[..., :half]
    second_half = values[..., half:]
    return jnp.concatenate(
        [first_half * cosine - second_half * sine, second_half * cosine + first_half * sine],
        axis=-1,
    )


def select_codes(codes, adapter, projections, adapters):
    count = codes.shape[0]
    width = codes.shape[1] // (adapters * projections)
    shaped = codes.reshape(count, adapters, projections, width)
    onehot = (adapter[:, None] == jnp.arange(adapters, dtype=jnp.int32)[None, :]).astype(
        codes.dtype
    )
    kept = shaped * onehot[:, :, None, None]
    return [kept[:, :, slot, :].reshape(count, adapters * width) for slot in range(projections)]


def add_adapter(partial_out, adapter_cols, offset, own_width):
    current = lax.dynamic_slice_in_dim(partial_out, offset, own_width, 1)
    return lax.dynamic_update_slice_in_dim(partial_out, current + adapter_cols, offset, 1)


def per_device(
    residual,
    pre_gain,
    query_weight,
    key_weight,
    value_weight,
    output_weight,
    adapter_down,
    adapter_up_query,
    adapter_up_key,
    adapter_up_value,
    adapter_down_out,
    adapter_up_out,
    post_gain,
    sink_logits,
    prompt_lengths,
    prompt_adapters,
):
    tok_rows = residual.shape[0]
    first = lax.axis_index("wide") * tok_rows
    member, prompt, position = token_layout(prompt_lengths, tok_rows, first)
    adapter = jnp.sum(member * prompt_adapters[None, :], axis=1)
    stream = residual.astype(jnp.float32)
    scale_rows = lax.rsqrt(jnp.mean(stream * stream, axis=1, keepdims=True) + epsilon)
    normed = (stream * scale_rows * pre_gain.astype(jnp.float32)[None, :]).astype(jnp.bfloat16)
    query_cols = query_weight.shape[1]
    key_cols = key_weight.shape[1]
    pieces = (
        lax.all_gather(query_weight, "wide", axis=0, tiled=True),
        lax.all_gather(key_weight, "wide", axis=0, tiled=True),
        lax.all_gather(value_weight, "wide", axis=0, tiled=True),
        lax.all_gather(adapter_down, "wide", axis=0, tiled=True),
    )
    query_part, key_part, value_part, code_part = tuple(
        (jnp.dot(normed, piece, preferred_element_type=jnp.float32) for piece in pieces)
    )
    codes = lax.all_gather(code_part.astype(jnp.bfloat16), "narrow", axis=1, tiled=True)
    chosen = select_codes(codes, adapter, 3, ADAPTERS)
    query = query_part + adapter_scale * jnp.dot(
        chosen[0], adapter_up_query, preferred_element_type=jnp.float32
    )
    key = key_part + adapter_scale * jnp.dot(
        chosen[1], adapter_up_key, preferred_element_type=jnp.float32
    )
    value = value_part + adapter_scale * jnp.dot(
        chosen[2], adapter_up_value, preferred_element_type=jnp.float32
    )
    local_heads = query_cols // HEAD_DIM
    local_kv = key_cols // HEAD_DIM
    group = local_heads // local_kv
    queries = (
        rotate(query.reshape(tok_rows, local_heads, HEAD_DIM), position)
        .astype(jnp.bfloat16)
        .reshape(tok_rows, local_kv, group, HEAD_DIM)
    )
    keys = rotate(key.reshape(tok_rows, local_kv, HEAD_DIM), position).astype(jnp.bfloat16)
    values = value.astype(jnp.bfloat16).reshape(tok_rows, local_kv, HEAD_DIM)
    sinks = sink_logits.reshape(local_kv, group)
    own_places = first + jnp.arange(tok_rows, dtype=jnp.int32)
    start_top = jnp.broadcast_to(sinks[None, :, :], (tok_rows, local_kv, group))
    start_total = jnp.ones((tok_rows, local_kv, group), jnp.float32)
    start_sum = jnp.zeros((tok_rows, local_kv, group, HEAD_DIM), jnp.float32)
    top = start_top
    total = start_total
    summed_values = start_sum
    piece_keys = lax.all_gather(keys, "wide", axis=0, tiled=True)
    piece_values = lax.all_gather(values, "wide", axis=0, tiled=True)
    count = piece_keys.shape[0]
    unused, key_prompt, unused_position = token_layout(prompt_lengths, count, jnp.int32(0))
    key_places = jnp.arange(count, dtype=jnp.int32)
    allowed = jnp.logical_and(
        prompt[:, None] == key_prompt[None, :], own_places[:, None] >= key_places[None, :]
    )[:, None, None, :]
    scores = (
        jnp.einsum("qgjd,kgd->qgjk", queries, piece_keys, preferred_element_type=jnp.float32)
        * score_scale
    )
    scores = jnp.where(allowed, scores, -1e30)
    fresh = jnp.maximum(top, jnp.max(scores, axis=-1))
    factor = jnp.exp(top - fresh)
    weights = jnp.where(allowed, jnp.exp(scores - fresh[..., None]), 0.0)
    total = total * factor + jnp.sum(weights, axis=-1)
    update = jnp.einsum(
        "qgjk,kgd->qgjd",
        weights.astype(jnp.bfloat16),
        piece_values,
        preferred_element_type=jnp.float32,
    )
    top, total, summed_values = (fresh, total, summed_values * factor[..., None] + update)
    attended = (
        (summed_values / total[..., None])
        .reshape(tok_rows, local_heads * HEAD_DIM)
        .astype(jnp.bfloat16)
    )
    code_terms = jnp.dot(attended, adapter_down_out, preferred_element_type=jnp.float32)
    codes_out = lax.psum(code_terms.astype(jnp.bfloat16), "narrow")
    chosen_out = select_codes(codes_out, adapter, 1, ADAPTERS)[0]
    adapter_cols = adapter_scale * jnp.dot(
        chosen_out, adapter_up_out, preferred_element_type=jnp.float32
    )
    own_width = adapter_up_out.shape[1]
    offset = lax.axis_index("narrow") * own_width
    partial_out = jnp.dot(
        attended,
        lax.all_gather(output_weight, "wide", axis=1, tiled=True),
        preferred_element_type=jnp.float32,
    )
    partial_out = add_adapter(partial_out, adapter_cols, offset, own_width)
    whole = lax.psum(partial_out.astype(jnp.bfloat16), "narrow").astype(jnp.float32)
    mean_square = jnp.mean(whole * whole, axis=1)
    projected = lax.dynamic_slice_in_dim(whole, offset, own_width, 1)
    factor_rows = lax.rsqrt(mean_square + epsilon)
    own_stream = lax.dynamic_slice_in_dim(stream, offset, own_width, 1)
    mixed = own_stream + projected * factor_rows[:, None] * post_gain.astype(jnp.float32)[None, :]
    return mixed.astype(jnp.bfloat16)


def solution(mesh):
    return jax.shard_map(
        per_device,
        mesh=mesh,
        in_specs=(
            P("wide", None),
            P(),
            P("wide", "narrow"),
            P("wide", "narrow"),
            P("wide", "narrow"),
            P("narrow", "wide"),
            P("wide", "narrow"),
            P(None, "narrow"),
            P(None, "narrow"),
            P(None, "narrow"),
            P("narrow", None),
            P(None, "narrow"),
            P("narrow"),
            P("narrow"),
            P(),
            P(),
        ),
        out_specs=P("wide", "narrow"),
        check_vma=False,
    )
```

profile of v0, /device:TPU:2, one launch (start us, length us, event | category | flops | bytes accessed | tf_op | source)
XLA Modules:
  0.0 509.5 jit_solution(2858889382094123757)
XLA Ops:
  6.5 0.7 all-gather.7.cloned.1.call-update
  7.3 0.0 all-gather.13.cloned.1.call-start
  7.3 0.7 all-gather.13.cloned.1.call-update
  8.0 0.0 all-gather.11.cloned.1.call-start
  8.1 0.7 all-gather.11.cloned.1.call-update
  8.7 0.0 all-gather.9.cloned.1.call-start
  8.8 0.7 convert_element_type.59
  9.5 0.8 reduce-window.8
  10.3 0.7 bitcast_subtract_fusion
  11.0 0.7 select_reduce_fusion.3
  11.8 25.8 %all_gather.25 = bf16[4608,96]{1,0:T(8,128)(2,1)S(1)} all-gather(bf16[144,96]{1,0:T(8,128)(2,1)} %param.22), channel_id=1, replica_groups=mesh['wide'=32,'narrow'=8] {'wide'}, dimensions={0}, use_global_device_ids=true | all-gather | bytes 912384 | tf_op jit(solution)/shard_map/all_gather | solution.py:89
  37.6 2.4 multiply_reduce_fusion.1
  40.0 2.7 convolution_convert_fusion.1
  42.6 28.5 %all_gather.26 = bf16[256,768]{0,1:T(8,128)(2,1)S(1)} all-gather(bf16[256,96]{0,1:T(8,128)(2,1)S(1)} %convolution_convert_fusion.1), channel_id=1, replica_groups=mesh['wide'=32,'narrow'=8] {'narrow'}, dimensions={1}, use_global_device_ids=true | all-gather | bytes 442368 | tf_op jit(solution)/shard_map/all_gather | solution.py:94
  71.2 0.5 multiply_cosine_fusion
  71.8 0.7 fusion.50
  72.5 2.9 fusion.49
  75.4 0.2 fusion.23
  75.6 0.7 fusion.51
  76.3 0.1 copy.44
  76.5 1.0 copy.45
  77.5 0.1 subtract_convert_fusion.1
  77.6 0.8 pad_maximum_fusion
  78.4 0.0 all-gather.9.cloned.1.call-update
  78.4 0.0 all-gather.15.cloned.1.call-start
  78.5 34.0 %all-gather.13.cloned.1.call-done = bf16[4608,256]{1,0:T(8,128)(2,1)} async-done(((bf16[144,256]{1,0:T(8,128)(2,1)}), bf16[4608,256]{1,0:T(8,128)(2,1)}) %all-gather.13.cloned.1.call-update) | async-done | bytes 2359312 | tf_op jit(solution)/shard_map/all_gather | solution.py:88
  112.4 2.9 fusion.47
  115.4 0.9 fusion.24
  116.2 0.0 all-gather.15.cloned.1.call-update
  116.3 0.0 all-gather.17.cloned.1.call-start
  116.3 0.5 all-gather.17.cloned.1.call-update
  116.8 0.2 all-reduce.3.cloned.1.call-start
  117.1 0.2 select_reduce_fusion
  117.3 0.1 broadcast_in_dim.20
  117.4 0.8 copy.37
  118.1 4.6 fusion.6
  122.8 43.2 %all-gather.11.cloned.1.call-done = bf16[4608,512]{1,0:T(8,128)(2,1)} async-done(((bf16[144,512]{1,0:T(8,128)(2,1)}), bf16[4608,512]{1,0:T(8,128)(2,1)}) %all-gather.11.cloned.1.call-update) | async-done | bytes 4718608 | tf_op jit(solution)/shard_map/all_gather | solution.py:86
  165.9 3.8 fusion.48
  169.7 1.0 fusion.11
  170.8 1.2 reshape.200
  172.0 0.5 subtract_convert_fusion
  172.5 46.5 %all-gather.9.cloned.1.call-done = bf16[8192,2,128]{2,0,1:T(8,128)(2,1)} async-done(((bf16[256,2,128]{2,0,1:T(8,128)(2,1)}), bf16[8192,2,128]{2,0,1:T(8,128)(2,1)}) %all-gather.9.cloned.1.call-update) | async-done | bytes 4194320 | tf_op jit(solution)/shard_map/all_gather | solution.py:123
  219.0 16.1 %fusion = (f32[256,2,2]{0,2,1:T(2,128)S(1)}, f32[2,8192,256,2]{2,1,3,0:T(8,128)}) fusion(pred[256,8192]{0,1:T(8,128)(4,1)} %fusion.6, bf16[256,2,2,64]{3,0,2,1:T(8,128)(2,1)S(1)} %bitcast.85, bf16[256,2,2,64]{3,0,2,1:T(8,128)(2,1)S(1)} %bitcast.84, bf16[8192,2,128]{2,0,1:T(8,128)(2,1)} %all-gather.9.cloned.1.call-done), kind=kOutput, calls=%fused_computation.2 | convolution fusion | flops 2173172736 | bytes 40112128 | tf_op jit(solution)/shard_map/qgjd,kgd->qgjk/dot_general | solution.py:132
  235.1 0.1 broadcast_maximum_fusion
  235.2 15.0 %fusion.1 = f32[256,2,2]{0,2,1:T(2,128)S(1)} fusion(f32[2,8192,256,2]{2,1,3,0:T(8,128)} %get-tuple-element.22, f32[256,2,2]{0,2,1:T(2,128)S(1)} %broadcast_maximum_fusion, pred[256,8192]{0,1:T(8,128)(4,1)S(1)} %copy-done.2), kind=kLoop, calls=%fused_computation.3 | loop fusion | flops 41942016 | bytes 35659776 | tf_op jit(solution)/shard_map/reduce_sum | solution.py:139
  250.2 0.1 fusion.42
  250.3 24.1 %all-gather.15.cloned.1.call-done = bf16[8192,2,128]{0,2,1:T(8,128)(2,1)} async-done(((bf16[256,2,128]{0,2,1:T(8,128)(2,1)}), bf16[8192,2,128]{0,2,1:T(8,128)(2,1)}) %all-gather.15.cloned.1.call-update) | async-done | bytes 4194320 | tf_op jit(solution)/shard_map/all_gather | solution.py:124
  274.4 15.9 %fusion.30 = bf16[256,2,2,128]{0,3,2,1:T(8,128)(2,1)S(1)} fusion(f32[2,8192,256,2]{2,1,3,0:T(8,128)} %get-tuple-element.22, f32[256,2,2]{0,2,1:T(2,128)S(1)} %broadcast_maximum_fusion, pred[256,8192]{0,1:T(8,128)(4,1)} %fusion.6, bf16[8192,2,128]{0,2,1:T(8,128)(2,1)} %all-gather.15.cloned.1.call-done, f32[256,2,2]{0,2,1:T(2,128)S(1)} %get-tuple-element.18, ...), kind=kOutput, calls=%fused_computation.29 | convolution fusion | flops 2189819904 | bytes 40120320 | tf_op jit(solution)/shard_map/qgjk,kgd->qgjd/dot_general | solution.py:140
  290.3 0.9 convolution_convert_fusion
  291.3 0.0 all-reduce.3.cloned.1.call-update
  291.3 0.3 all-reduce.5.cloned.1.call-start
  291.6 36.4 %all-gather.17.cloned.1.call-done = bf16[512,4608]{0,1:T(8,128)(2,1)} async-done(((bf16[512,144]{0,1:T(8,128)(2,1)}), bf16[512,4608]{0,1:T(8,128)(2,1)}) %all-gather.17.cloned.1.call-update) | async-done | bytes 4718608 | tf_op jit(solution)/shard_map/all_gather | solution.py:162
  328.0 5.9 %fusion.52 = f32[256,4608]{1,0:T(8,128)} fusion(bf16[256,512]{0,1:T(8,128)(2,1)S(1)} %bitcast.77, bf16[512,4608]{0,1:T(8,128)(2,1)} %all-gather.17.cloned.1.call-done), kind=kOutput, calls=%fused_computation.72 | convolution fusion | flops 1207959552 | bytes 9699328 | tf_op jit(solution)/shard_map/dot_general | solution.py:160
  333.9 68.7 %all-reduce.3.cloned.1.call-done = bf16[256,256]{1,0:T(8,128)(2,1)} async-done(((bf16[256,256]{1,0:T(8,128)(2,1)}), bf16[256,256]{1,0:T(8,128)(2,1)}) %all-reduce.3.cloned.1.call-update) | async-done | bytes 131088 | tf_op jit(solution)/shard_map/psum | solution.py:153
  402.6 1.5 fusion.10
  404.2 4.5 dynamic_update_slice.3
  408.7 4.0 convert_element_type.69
  412.7 0.0 all-reduce.5.cloned.1.call-update
  412.7 2.7 convert_element_type.58
  415.4 80.3 %all-reduce.5.cloned.1.call-done = bf16[256,4608]{1,0:T(8,128)(2,1)} async-done(((bf16[256,4608]{1,0:T(8,128)(2,1)}), bf16[256,4608]{1,0:T(8,128)(2,1)}) %all-reduce.5.cloned.1.call-update) | async-done | bytes 2359312 | tf_op jit(solution)/shard_map/psum | solution.py:166
  495.7 2.2 multiply_reduce_fusion
  497.9 2.2 convert_element_type.70
  500.1 1.6 add_convert_fusion
  501.7 0.9 copy.39
  (37 shorter events, 0.2 us)
Async XLA Ops:
  6.5 396.1 %copy-start = (bf16[256,576]{0,1:T(8,128)(2,1)S(1)}, bf16[256,576]{0,1:T(8,128)(2,1)}, u32[]{:S(2)}) copy-start(bf16[256,576]{0,1:T(8,128)(2,1)} %param.27) | copy-start | bytes 884740
  6.5 65.9 %all-gather.7.cloned.1.call-start = ((), (), s32[]{:S(2)}) async-start(), calls=%async_computation | async-start | bytes 2433024 | tf_op jit(solution)/shard_map/all_gather | solution.py:87
  7.3 105.2 %all-gather.13.cloned.1.call-start = ((), (), s32[]{:S(2)}) async-start(), calls=%async_computation.3 | async-start | bytes 2433024 | tf_op jit(solution)/shard_map/all_gather | solution.py:88
  8.0 157.9 %all-gather.11.cloned.1.call-start = ((), (), s32[]{:S(2)}) async-start(), calls=%async_computation.2 | async-start | bytes 4866048 | tf_op jit(solution)/shard_map/all_gather | solution.py:86
  8.7 210.3 %all-gather.9.cloned.1.call-start = ((), (), s32[]{:S(2)}) async-start(), calls=%async_computation.1 | async-start | bytes 4325376 | tf_op jit(solution)/shard_map/all_gather | solution.py:123
  37.6 34.9 %copy-start.1 = (bf16[256,4608]{1,0:T(8,128)(2,1)S(1)}, bf16[256,4608]{1,0:T(8,128)(2,1)}, u32[]{:S(2)}) copy-start(bf16[256,4608]{1,0:T(8,128)(2,1)} %param.16) | copy-start | bytes 7077892
  42.6 32.8 %copy-start.9 = (bf16[256,256]{1,0:T(8,128)(2,1)S(1)}, bf16[256,256]{1,0:T(8,128)(2,1)}, u32[]{:S(2)}) copy-start(bf16[256,256]{1,0:T(8,128)(2,1)} %param.24) | copy-start | bytes 393220
  76.5 40.8 %copy-start.11 = (f32[4]{0:T(128)S(1)}, f32[4]{0:T(128)}, u32[]{:S(2)}) copy-start(f32[4]{0:T(128)} %param.29) | copy-start | bytes 52
  77.6 37.7 %copy-start.4 = (bf16[256,16,1,16]{0,3,2,1:T(8,128)(2,1)S(1)}, bf16[256,16,1,16]{0,3,2,1:T(8,128)(2,1)}, u32[]{:S(2)}) copy-start(bf16[256,16,1,16]{0,3,2,1:T(8,128)(2,1)} %get-tuple-element.12) | copy-start | bytes 393220
  77.6 37.7 %copy-start.8 = (bf16[256,256]{1,0:T(8,128)(2,1)S(1)}, bf16[256,256]{1,0:T(8,128)(2,1)}, u32[]{:S(2)}) copy-start(bf16[256,256]{1,0:T(8,128)(2,1)} %param.25) | copy-start | bytes 393220
  78.4 196.0 %all-gather.15.cloned.1.call-start = ((), (), s32[]{:S(2)}) async-start(), calls=%async_computation.4 | async-start | bytes 4325376 | tf_op jit(solution)/shard_map/all_gather | solution.py:124
  116.3 211.7 %all-gather.17.cloned.1.call-start = ((), (), s32[]{:S(2)}) async-start(), calls=%async_computation.5 | async-start | bytes 4866048 | tf_op jit(solution)/shard_map/all_gather | solution.py:162
  116.8 285.8 %all-reduce.3.cloned.1.call-start = ((), (), s32[]{:S(2)}) async-start(), calls=%async_computation.6 | async-start | bytes 262144 | tf_op jit(solution)/shard_map/psum | solution.py:153
  122.8 46.9 %copy-start.5 = (bf16[256,16,1,16]{0,3,2,1:T(8,128)(2,1)S(1)}, bf16[256,16,1,16]{0,3,2,1:T(8,128)(2,1)}, u32[]{:S(2)}) copy-start(bf16[256,16,1,16]{0,3,2,1:T(8,128)(2,1)} %get-tuple-element.13) | copy-start | bytes 393220
  122.8 46.9 %copy-start.7 = (bf16[256,512]{1,0:T(8,128)(2,1)S(1)}, bf16[256,512]{1,0:T(8,128)(2,1)}, u32[]{:S(2)}) copy-start(bf16[256,512]{1,0:T(8,128)(2,1)} %param.23) | copy-start | bytes 786436
  219.0 16.2 %copy-start.2 = (pred[256,8192]{0,1:T(8,128)(4,1)S(1)}, pred[256,8192]{0,1:T(8,128)(4,1)}, u32[]{:S(2)}) copy-start(pred[256,8192]{0,1:T(8,128)(4,1)} %fusion.6) | copy-start | bytes 6291460
  274.4 15.9 %copy-start.6 = (bf16[512,256]{1,0:T(8,128)(2,1)S(1)}, bf16[512,256]{1,0:T(8,128)(2,1)}, u32[]{:S(2)}) copy-start(bf16[512,256]{1,0:T(8,128)(2,1)} %param.26) | copy-start | bytes 786436
  291.3 111.4 %copy-start.3 = (bf16[256,256]{1,0:T(8,128)(2,1)S(1)}, bf16[256,256]{1,0:T(8,128)(2,1)}, u32[]{:S(2)}) copy-start(bf16[256,256]{1,0:T(8,128)(2,1)} %copy.37) | copy-start | bytes 393220
  291.3 204.4 %all-reduce.5.cloned.1.call-start = ((), (), s32[]{:S(2)}) async-start(), calls=%async_computation.7 | async-start | bytes 4718592 | tf_op jit(solution)/shard_map/psum | solution.py:166
  412.7 2.7 copy-start.10
Sparse Core Ops, SparseCore 0:
  9.9 51.6 all-gather.6
  64.1 48.2 all-gather.12
  115.0 50.9 all-gather.10
  168.4 50.5 all-gather.8
  221.3 53.0 all-gather.14
  276.8 51.1 all-gather.16
  330.3 72.2 all-reduce.2
  412.8 82.8 all-reduce.4
where the time goes:
time: 510 us; the launch traced here: 509 us
  waiting for transfers between devices  336 us (66%)
  matrix products  54.8 us (11%)
  blocking collectives  54.3 us (11%)
  other arithmetic  39.9 us (8%)
  between operations  13.8 us (3%)
  local copies, waits for them, and re-layouts  10.1 us (2%)
    psum x1, waiting for transfers between devices, per_device(): lax.psum(partial_out.astype(jnp.bfloat16), 'narrow').astype(jnp.float32)  80.3 us
    psum x1, waiting for transfers between devices, per_device(): codes_out = lax.psum(code_terms.astype(jnp.bfloat16), 'narrow')  68.7 us
    all_gather x1, waiting for transfers between devices, per_device(): piece_keys = lax.all_gather(keys, 'wide', axis=0, tiled=True)  46.5 us
    all_gather x1, waiting for transfers between devices, per_device(): lax.all_gather(query_weight, 'wide', axis=0, tiled=True)  43.2 us
    all_gather x1, waiting for transfers between devices, per_device(): lax.all_gather(output_weight, 'wide', axis=1, tiled=True)  36.4 us
    all_gather x1, waiting for transfers between devices, per_device(): lax.all_gather(value_weight, 'wide', axis=0, tiled=True)  34 us
    all_gather x1, blocking collectives, per_device(): lax.all_gather(code_part.astype(jnp.bfloat16), 'narrow', axis=1, tiled=True)  28.5 us
    all_gather x1, blocking collectives, per_device(): lax.all_gather(adapter_down, 'wide', axis=0, tiled=True)  25.8 us
  transfers between devices with their start and end apart: 8, of which 7 were waited for; matrix products, arithmetic and copies ran while one was open for 17% of the time, Pallas kernels for 0%

commit v1 on v0

--- a/solution.py
+++ b/solution.py
@@ -120,7 +120,9 @@
     top = start_top
     total = start_total
     summed_values = start_sum
-    piece_keys = lax.all_gather(keys, "wide", axis=0, tiled=True)
+    piece_keys = jnp.concatenate(
+        lax.all_to_all(jnp.stack([keys] * lax.axis_size("wide")), "wide", 0, 0), axis=0
+    )
     piece_values = lax.all_gather(values, "wide", axis=0, tiled=True)
     count = piece_keys.shape[0]
     unused, key_prompt, unused_position = token_layout(prompt_lengths, count, jnp.int32(0))

time: 510 us -> 485 us (0.951)
  waiting for transfers between devices: 336 us -> 298 us
  local copies, waits for them, and re-layouts: 10.1 us -> 16.7 us
  starting transfers between devices: 0.68 us -> 6.6 us
    all_gather x1 -> x0, waiting for transfers between devices: 46.5 us -> none  [per_device(): piece_keys = lax.all_gather(keys, 'wide', axis=0, tiled=True)]
    all_to_all x0 -> x1, waiting for transfers between devices: none -> 45 us  [per_device(): lax.all_to_all(jnp.stack([keys] * lax.axis_size('wide')), 'wide', 0, 0)]
    all_gather x1, waiting for transfers between devices: 0.01 us -> 36.4 us  [per_device(): lax.all_gather(key_weight, 'wide', axis=0, tiled=True)]
    all_gather x1, waiting for transfers between devices: 34 us -> 0.01 us  [per_device(): lax.all_gather(value_weight, 'wide', axis=0, tiled=True)]
    all_gather x1, waiting for transfers between devices: 43.2 us -> 11.9 us  [per_device(): lax.all_gather(query_weight, 'wide', axis=0, tiled=True)]
    all_gather x1, waiting for transfers between devices: 24.1 us -> 17.4 us  [per_device(): piece_values = lax.all_gather(values, 'wide', axis=0, tiled=True)]
    all_to_all x0 -> x1, starting transfers between devices: none -> 5.96 us  [per_device(): lax.all_to_all(jnp.stack([keys] * lax.axis_size('wide')), 'wide', 0, 0)]
  transfers between devices with their start and end apart: 8 -> 8, of which waited for: 7 -> 7; matrix products, arithmetic and copies ran while one was open for 17% -> 19% of each run, Pallas kernels for 0% -> 0%
where the time goes in v1:
time: 485 us; the launch traced here: 484 us
  waiting for transfers between devices  298 us (61%)
  matrix products  54.9 us (11%)
  blocking collectives  54.4 us (11%)
  other arithmetic  39 us (8%)
  local copies, waits for them, and re-layouts  16.7 us (3%)
  between operations  13.8 us (3%)
  starting transfers between devices  6.6 us (1%)
    psum x1, waiting for transfers between devices, per_device(): lax.psum(partial_out.astype(jnp.bfloat16), 'narrow').astype(jnp.float32)  80.1 us
    psum x1, waiting for transfers between devices, per_device(): codes_out = lax.psum(code_terms.astype(jnp.bfloat16), 'narrow')  68.6 us
    all_to_all x1, waiting for transfers between devices, per_device(): lax.all_to_all(jnp.stack([keys] * lax.axis_size('wide')), 'wide', 0, 0)  45 us
    all_gather x1, waiting for transfers between devices, per_device(): lax.all_gather(output_weight, 'wide', axis=1, tiled=True)  36.5 us
    all_gather x1, waiting for transfers between devices, per_device(): lax.all_gather(key_weight, 'wide', axis=0, tiled=True)  36.4 us
    all_gather x1, blocking collectives, per_device(): lax.all_gather(code_part.astype(jnp.bfloat16), 'narrow', axis=1, tiled=True)  28.6 us
    all_gather x1, blocking collectives, per_device(): lax.all_gather(adapter_down, 'wide', axis=0, tiled=True)  25.8 us
    all_gather x1, waiting for transfers between devices, per_device(): piece_values = lax.all_gather(values, 'wide', axis=0, tiled=True)  17.4 us
  transfers between devices with their start and end apart: 8, of which 7 were waited for; matrix products, arithmetic and copies ran while one was open for 19% of the time, Pallas kernels for 0%

profile of v1, /device:TPU:2, one launch (start us, length us, event | category | flops | bytes accessed | tf_op | source)
XLA Modules:
  0.0 483.7 jit_solution(4400907730138677800)
XLA Ops:
  6.5 0.7 all-gather.10.cloned.1.call-update
  7.3 0.0 all-gather.6.cloned.1.call-start
  7.3 0.7 all-gather.6.cloned.1.call-update
  8.0 0.0 all-gather.8.cloned.1.call-start
  8.1 0.7 all-gather.8.cloned.1.call-update
  8.7 0.0 all-gather.12.cloned.1.call-start
  8.8 0.7 convert_element_type.61
  9.5 0.8 reduce-window.8
  10.3 0.7 bitcast_subtract_fusion
  11.0 0.7 select_reduce_fusion.3
  11.7 25.8 %all_gather.22 = bf16[4608,96]{1,0:T(8,128)(2,1)S(1)} all-gather(bf16[144,96]{1,0:T(8,128)(2,1)} %param.22), channel_id=1, replica_groups=mesh['wide'=32,'narrow'=8] {'wide'}, dimensions={0}, use_global_device_ids=true | all-gather | bytes 912384 | tf_op jit(solution)/shard_map/all_gather | solution.py:89
  37.5 2.4 multiply_reduce_fusion.1
  39.9 2.7 convolution_convert_fusion.1
  42.6 0.0 copy-start.7
  42.6 28.6 %all_gather.23 = bf16[256,768]{0,1:T(8,128)(2,1)S(1)} all-gather(bf16[256,96]{0,1:T(8,128)(2,1)S(1)} %convolution_convert_fusion.1), channel_id=1, replica_groups=mesh['wide'=32,'narrow'=8] {'narrow'}, dimensions={1}, use_global_device_ids=true | all-gather | bytes 442368 | tf_op jit(solution)/shard_map/all_gather | solution.py:94
  71.2 0.7 fusion.49
  71.9 2.9 fusion.46
  74.8 0.9 fusion.22
  75.7 0.0 all-gather.12.cloned.1.call-update
  75.8 0.3 multiply_cosine_fusion
  76.1 36.4 %all-gather.6.cloned.1.call-done = bf16[4608,256]{1,0:T(8,128)(2,1)} async-done(((bf16[144,256]{1,0:T(8,128)(2,1)}), bf16[4608,256]{1,0:T(8,128)(2,1)}) %all-gather.6.cloned.1.call-update) | async-done | bytes 2359312 | tf_op jit(solution)/shard_map/all_gather | solution.py:87
  112.5 2.9 fusion.48
  115.4 0.2 fusion.21
  115.7 0.1 copy.44
  115.8 3.0 stack.2
  118.9 6.0 %all-to-all-start = ((bf16[32,256,2,128]{3,1,2,0:T(8,128)(2,1)}), bf16[32,256,2,128]{3,1,2,0:T(8,128)(2,1)}, u32[]{:S(2)}, u32[]{:S(2)}) async-start(bf16[32,256,2,128]{3,1,2,0:T(8,128)(2,1)} %stack.2), calls=%async_computation | async-start | bytes 8388608 | tf_op jit(solution)/shard_map/all_to_all | solution.py:124
  124.8 0.0 all-gather.14.cloned.1.call-start
  124.9 0.5 all-gather.14.cloned.1.call-update
  125.4 0.2 all-reduce.3.cloned.1.call-start
  125.6 0.1 copy.46
  125.7 0.1 copy.47
  125.8 0.1 broadcast_in_dim.20
  125.9 0.8 copy.51
  126.7 0.2 select_reduce_fusion
  126.9 4.7 fusion.6
  131.6 45.0 %all-to-all-done = bf16[32,256,2,128]{3,1,2,0:T(8,128)(2,1)} async-done(((bf16[32,256,2,128]{3,1,2,0:T(8,128)(2,1)}), bf16[32,256,2,128]{3,1,2,0:T(8,128)(2,1)}, u32[]{:S(2)}, u32[]{:S(2)}) %all-to-all-start) | async-done | bytes 4194336 | tf_op jit(solution)/shard_map/all_to_all | solution.py:124
  176.6 5.1 %copy.45 = bf16[32,256,2,128]{3,1,0,2:T(8,128)(2,1)} copy(bf16[32,256,2,128]{3,1,2,0:T(8,128)(2,1)} %all-to-all-done) | data formatting | bytes 8388608 | tf_op jit(solution)/shard_map/all_to_all | solution.py:124
  181.6 11.9 %all-gather.8.cloned.1.call-done = bf16[4608,512]{1,0:T(8,128)(2,1)} async-done(((bf16[144,512]{1,0:T(8,128)(2,1)}), bf16[4608,512]{1,0:T(8,128)(2,1)}) %all-gather.8.cloned.1.call-update) | async-done | bytes 4718608 | tf_op jit(solution)/shard_map/all_gather | solution.py:86
  193.5 3.8 fusion.47
  197.4 1.1 fusion.9
  198.4 1.2 reshape.211
  199.6 0.5 subtract_convert_fusion
  200.2 16.1 %fusion = (f32[256,2,2]{0,2,1:T(2,128)S(1)}, f32[2,8192,256,2]{2,1,3,0:T(8,128)}) fusion(pred[256,8192]{0,1:T(8,128)(4,1)} %fusion.6, bf16[8192,2,128,1]{2,0,3,1:T(8,128)(2,1)} %bitcast.74, bf16[256,2,2,64]{3,0,2,1:T(8,128)(2,1)S(1)} %bitcast.84, bf16[256,2,2,64]{3,0,2,1:T(8,128)(2,1)S(1)} %bitcast.85), kind=kOutput, calls=%fused_computation.2 | convolution fusion | flops 2173172736 | bytes 40112128 | tf_op jit(solution)/shard_map/qgjd,kgd->qgjk/dot_general | solution.py:134
  216.3 0.1 broadcast_maximum_fusion
  216.4 15.0 %fusion.1 = f32[256,2,2]{0,2,1:T(2,128)S(1)} fusion(f32[2,8192,256,2]{2,1,3,0:T(8,128)} %get-tuple-element.20, f32[256,2,2]{0,2,1:T(2,128)S(1)} %broadcast_maximum_fusion, pred[256,8192]{0,1:T(8,128)(4,1)S(1)} %copy-done.2), kind=kLoop, calls=%fused_computation.3 | loop fusion | flops 41942016 | bytes 35659776 | tf_op jit(solution)/shard_map/reduce_sum | solution.py:141
  231.4 0.1 fusion.41
  231.5 17.4 %all-gather.12.cloned.1.call-done = bf16[8192,2,128]{0,2,1:T(8,128)(2,1)} async-done(((bf16[256,2,128]{0,2,1:T(8,128)(2,1)}), bf16[8192,2,128]{0,2,1:T(8,128)(2,1)}) %all-gather.12.cloned.1.call-update) | async-done | bytes 4194320 | tf_op jit(solution)/shard_map/all_gather | solution.py:126
  248.9 16.0 %fusion.28 = bf16[256,2,2,128]{0,3,2,1:T(8,128)(2,1)S(1)} fusion(f32[2,8192,256,2]{2,1,3,0:T(8,128)} %get-tuple-element.20, f32[256,2,2]{0,2,1:T(2,128)S(1)} %broadcast_maximum_fusion, pred[256,8192]{0,1:T(8,128)(4,1)} %fusion.6, bf16[8192,2,128]{0,2,1:T(8,128)(2,1)} %all-gather.12.cloned.1.call-done, f32[256,2,2]{0,2,1:T(2,128)S(1)} %get-tuple-element.16, ...), kind=kOutput, calls=%fused_computation.27 | convolution fusion | flops 2189819904 | bytes 40120320 | tf_op jit(solution)/shard_map/qgjk,kgd->qgjd/dot_general | solution.py:142
  264.9 0.9 convolution_convert_fusion
  265.8 0.0 all-reduce.3.cloned.1.call-update
  265.9 0.3 all-reduce.5.cloned.1.call-start
  266.1 36.5 %all-gather.14.cloned.1.call-done = bf16[512,4608]{0,1:T(8,128)(2,1)} async-done(((bf16[512,144]{0,1:T(8,128)(2,1)}), bf16[512,4608]{0,1:T(8,128)(2,1)}) %all-gather.14.cloned.1.call-update) | async-done | bytes 4718608 | tf_op jit(solution)/shard_map/all_gather | solution.py:164
  302.6 5.9 %fusion.50 = f32[256,4608]{1,0:T(8,128)} fusion(bf16[256,512]{0,1:T(8,128)(2,1)S(1)} %bitcast.77, bf16[512,4608]{0,1:T(8,128)(2,1)} %all-gather.14.cloned.1.call-done), kind=kOutput, calls=%fused_computation.70 | convolution fusion | flops 1207959552 | bytes 9699328 | tf_op jit(solution)/shard_map/dot_general | solution.py:162
  308.5 68.6 %all-reduce.3.cloned.1.call-done = bf16[256,256]{1,0:T(8,128)(2,1)} async-done(((bf16[256,256]{1,0:T(8,128)(2,1)}), bf16[256,256]{1,0:T(8,128)(2,1)}) %all-reduce.3.cloned.1.call-update) | async-done | bytes 131088 | tf_op jit(solution)/shard_map/psum | solution.py:155
  377.1 1.5 fusion.8
  378.6 4.5 dynamic_update_slice.3
  383.1 4.0 convert_element_type.71
  387.2 0.0 all-reduce.5.cloned.1.call-update
  387.2 2.7 convert_element_type.60
  389.9 80.1 %all-reduce.5.cloned.1.call-done = bf16[256,4608]{1,0:T(8,128)(2,1)} async-done(((bf16[256,4608]{1,0:T(8,128)(2,1)}), bf16[256,4608]{1,0:T(8,128)(2,1)}) %all-reduce.5.cloned.1.call-update) | async-done | bytes 2359312 | tf_op jit(solution)/shard_map/psum | solution.py:168
  470.0 2.2 multiply_reduce_fusion
  472.2 2.2 convert_element_type.72
  474.4 1.6 add_convert_fusion
  476.0 0.9 copy.53
  (36 shorter events, 0.3 us)
Async XLA Ops:
  6.5 370.6 %copy-start = (bf16[256,576]{0,1:T(8,128)(2,1)S(1)}, bf16[256,576]{0,1:T(8,128)(2,1)}, u32[]{:S(2)}) copy-start(bf16[256,576]{0,1:T(8,128)(2,1)} %param.27) | copy-start | bytes 884740
  6.5 65.3 %all-gather.10.cloned.1.call-start = ((), (), s32[]{:S(2)}) async-start(), calls=%async_computation.3 | async-start | bytes 2433024 | tf_op jit(solution)/shard_map/all_gather | solution.py:88
  7.3 105.2 %all-gather.6.cloned.1.call-start = ((), (), s32[]{:S(2)}) async-start(), calls=%async_computation.1 | async-start | bytes 2433024 | tf_op jit(solution)/shard_map/all_gather | solution.py:87
  8.0 185.5 %all-gather.8.cloned.1.call-start = ((), (), s32[]{:S(2)}) async-start(), calls=%async_computation.2 | async-start | bytes 4866048 | tf_op jit(solution)/shard_map/all_gather | solution.py:86
  8.7 240.2 %all-gather.12.cloned.1.call-start = ((), (), s32[]{:S(2)}) async-start(), calls=%async_computation.4 | async-start | bytes 4325376 | tf_op jit(solution)/shard_map/all_gather | solution.py:126
  37.5 34.4 %copy-start.1 = (bf16[256,4608]{1,0:T(8,128)(2,1)S(1)}, bf16[256,4608]{1,0:T(8,128)(2,1)}, u32[]{:S(2)}) copy-start(bf16[256,4608]{1,0:T(8,128)(2,1)} %param.16) | copy-start | bytes 7077892
  42.6 32.3 %copy-start.7 = (bf16[256,256]{1,0:T(8,128)(2,1)S(1)}, bf16[256,256]{1,0:T(8,128)(2,1)}, u32[]{:S(2)}) copy-start(bf16[256,256]{1,0:T(8,128)(2,1)} %param.25) | copy-start | bytes 393220
  74.8 40.6 %copy-start.8 = (bf16[256,256]{1,0:T(8,128)(2,1)S(1)}, bf16[256,256]{1,0:T(8,128)(2,1)}, u32[]{:S(2)}) copy-start(bf16[256,256]{1,0:T(8,128)(2,1)} %param.24) | copy-start | bytes 393220
  118.9 7.0 %copy-start.10 = (f32[4]{0:T(128)S(1)}, f32[4]{0:T(128)}, u32[]{:S(2)}) copy-start(f32[4]{0:T(128)} %param.29) | copy-start | bytes 52
  118.9 57.7 %all-to-all-start = ((bf16[32,256,2,128]{3,1,2,0:T(8,128)(2,1)}), bf16[32,256,2,128]{3,1,2,0:T(8,128)(2,1)}, u32[]{:S(2)}, u32[]{:S(2)}) async-start(bf16[32,256,2,128]{3,1,2,0:T(8,128)(2,1)} %stack.2), calls=%async_computation | async-start | bytes 8388608 | tf_op jit(solution)/shard_map/all_to_all | solution.py:124
  124.8 177.8 %all-gather.14.cloned.1.call-start = ((), (), s32[]{:S(2)}) async-start(), calls=%async_computation.5 | async-start | bytes 4866048 | tf_op jit(solution)/shard_map/all_gather | solution.py:164
  125.4 251.7 %all-reduce.3.cloned.1.call-start = ((), (), s32[]{:S(2)}) async-start(), calls=%async_computation.6 | async-start | bytes 262144 | tf_op jit(solution)/shard_map/psum | solution.py:155
  193.5 3.8 copy-start.4
  193.5 3.8 copy-start.6
  200.2 16.2 %copy-start.2 = (pred[256,8192]{0,1:T(8,128)(4,1)S(1)}, pred[256,8192]{0,1:T(8,128)(4,1)}, u32[]{:S(2)}) copy-start(pred[256,8192]{0,1:T(8,128)(4,1)} %fusion.6) | copy-start | bytes 6291460
  248.9 16.0 %copy-start.5 = (bf16[512,256]{1,0:T(8,128)(2,1)S(1)}, bf16[512,256]{1,0:T(8,128)(2,1)}, u32[]{:S(2)}) copy-start(bf16[512,256]{1,0:T(8,128)(2,1)} %param.26) | copy-start | bytes 786436
  265.9 111.2 %copy-start.3 = (bf16[256,256]{1,0:T(8,128)(2,1)S(1)}, bf16[256,256]{1,0:T(8,128)(2,1)}, u32[]{:S(2)}) copy-start(bf16[256,256]{1,0:T(8,128)(2,1)} %copy.51) | copy-start | bytes 393220
  265.9 204.1 %all-reduce.5.cloned.1.call-start = ((), (), s32[]{:S(2)}) async-start(), calls=%async_computation.7 | async-start | bytes 4718592 | tf_op jit(solution)/shard_map/psum | solution.py:168
  387.1 2.7 copy-start.9
Sparse Core Ops, SparseCore 0:
  9.9 51.6 all-gather.9
  64.1 48.3 all-gather.5
  115.0 78.4 all-gather.7
  195.8 53.0 all-gather.11
  251.3 51.2 all-gather.13
  304.8 72.2 all-reduce.2
  387.3 82.6 all-reduce.4
